TPU v7x, 32 devices: a whole 2x2x4 slice. The times are simulated.
32 devices in a mesh: groups: 2 (over y), blk: 4 (over z), heads: 2 (over x), section: 2 (over core).
Axes of the slice: x: 2, y: 2, z: 4, core: 2. Of those that a mesh axis runs over, the one named last changes fastest.
Arguments:
- dec_states: bfloat16 [4096, 2304], P(('groups', 'blk', 'section')), parts along dimension 0, may hold values from -6 to 6
- cross_keys: bfloat16 [1024, 1, 256], P(('groups', 'blk')), parts along dimension 0, may hold values from -15 to 15
- cross_values: bfloat16 [1024, 1, 256], P(('groups', 'blk')), parts along dimension 0, may hold values from -6 to 6
- attn_gain: float32 [2304], replicated, may hold values from 0.1 to 1.9
- query_weight: bfloat16 [2304, 512], P(None, 'heads'), may hold values from -0.125 to 0.125
- out_weight: bfloat16 [512, 2304], P('heads'), may hold values from -0.25 to 0.25
- post_attn_gain: float32 [2304], replicated, may hold values from 0.1 to 1.9
- ffn_gain: float32 [2304], replicated, may hold values from 0.1 to 1.9
- gate_weight: bfloat16 [2304, 9216], P('blk', ('heads', 'section')), may hold values from -0.125 to 0.125
- up_weight: bfloat16 [2304, 9216], P('blk', ('heads', 'section')), may hold values from -0.125 to 0.125
- down_weight: bfloat16 [9216, 2304], P(('heads', 'section'), 'blk'), may hold values from -0.0625 to 0.0625
- post_ffn_gain: float32 [2304], replicated, may hold values from 0.1 to 1.9
Outputs:
- scored_states: bfloat16 [4096, 2304], P(('groups', 'blk', 'heads', 'section')), parts along dimension 0
There are 2 independent parts, one for each index of `groups`. A program takes and returns all parts, laid end to end along the dimension named above; an argument that names none is the same for every part. Nothing has to cross between parts.
All inputs are finite; a program needn't handle non-finite values.
Results may differ from a plain program's by a relative error of at most 0.02.
Values may be sent and summed in bfloat16 or wider, within the bound.
No kernel may reach another device: no remote copies, remote signals or barrier semaphores. Data moves between devices by JAX's collectives and lax.ppermute only.
A program may use at most 128 MiB of HBM per device.

v0:
```python
import jax
import jax.numpy as jnp
from jax import lax
from jax.sharding import PartitionSpec as P

HD = 256
GROUP = 2
softcap_limit = 50.0


def from_partner(block, axis, bit):
    count = lax.axis_size(axis)
    route = []
    for low in range(count):
        high = low | 1 << bit
        if high != low and high < count:
            route += [(low, high), (high, low)]
    return lax.ppermute(block, axis, route)


def rms_scale(values, gain):
    return values * lax.rsqrt(jnp.mean(values * values, axis=-1, keepdims=True) + 1e-06) * gain


def capped_scores(queries, keys):
    raw = lax.dot_general(
        queries, keys, (((1,), (1,)), ((), ())), preferred_element_type=jnp.float32
    ) * HD ** (-0.5)
    return softcap_limit * jnp.tanh(raw / softcap_limit)


def body(
    dec_states,
    cross_keys,
    cross_values,
    attn_gain,
    query_weight,
    out_weight,
    post_attn_gain,
    ffn_gain,
    gate_weight,
    up_weight,
    down_weight,
    post_ffn_gain,
):
    head_index = lax.axis_index("heads")
    kv_index = head_index // GROUP
    keys_local = lax.dynamic_index_in_dim(cross_keys, kv_index, 1, keepdims=False)
    values_local = lax.dynamic_index_in_dim(cross_values, kv_index, 1, keepdims=False)
    gate_full, up_full, down_full = (
        lax.all_gather(gate_weight, "blk", axis=0, tiled=True),
        lax.all_gather(up_weight, "blk", axis=0, tiled=True),
        lax.all_gather(down_weight, "blk", axis=1, tiled=True),
    )
    states = dec_states.astype(jnp.float32)
    normed = rms_scale(states, attn_gain).astype(jnp.bfloat16)
    queries = jnp.dot(normed, query_weight, preferred_element_type=jnp.float32).astype(jnp.bfloat16)
    rows_here = queries.shape[0]
    probs = jnp.exp(capped_scores(queries, lax.all_gather(keys_local, "blk", axis=0, tiled=True)))
    numer = jnp.dot(
        probs.astype(jnp.bfloat16),
        lax.all_gather(values_local, "blk", axis=0, tiled=True),
        preferred_element_type=jnp.float32,
    )
    numer, denom = (numer, jnp.sum(probs, axis=1))
    context = (numer / denom[:, None]).astype(jnp.bfloat16)
    head_term = jnp.dot(context, out_weight, preferred_element_type=jnp.float32)
    attended = lax.psum(head_term.astype(jnp.bfloat16), "heads").astype(jnp.float32)
    residual = (states + rms_scale(attended, post_attn_gain)).astype(jnp.bfloat16)
    ffn_input = rms_scale(residual.astype(jnp.float32), ffn_gain).astype(jnp.bfloat16)
    section_size = lax.axis_size("section")
    section_index = lax.axis_index("section")
    out_rows = rows_here // lax.axis_size("heads")
    block_index = head_index * section_size + section_index
    ffn_rows = lax.all_gather(ffn_input, "section", axis=0, tiled=True)
    partner_block = head_index * section_size + (1 - section_index)
    send_start = jnp.clip(
        partner_block * out_rows - section_index * rows_here, 0, rows_here - out_rows
    )
    outgoing = lax.dynamic_slice_in_dim(residual, send_start, out_rows, 0)
    incoming = from_partner(outgoing, "section", 0)
    own_start = jnp.clip(
        block_index * out_rows - section_index * rows_here, 0, rows_here - out_rows
    )
    local_rows = lax.dynamic_slice_in_dim(residual, own_start, out_rows, 0)
    holder = block_index * out_rows // rows_here
    residual_out = jnp.where(holder == section_index, local_rows, incoming)
    gate = jnp.dot(ffn_rows, gate_full, preferred_element_type=jnp.float32)
    up_part = jnp.dot(ffn_rows, up_full, preferred_element_type=jnp.float32)
    hidden = (jax.nn.gelu(gate, approximate=True) * up_part).astype(jnp.bfloat16)
    terms = jnp.dot(hidden, down_full, preferred_element_type=jnp.float32)
    ffn_out = lax.psum_scatter(
        terms.astype(jnp.bfloat16), ("heads", "section"), scatter_dimension=0, tiled=True
    ).astype(jnp.float32)
    return (residual_out.astype(jnp.float32) + rms_scale(ffn_out, post_ffn_gain)).astype(
        jnp.bfloat16
    )


def solution(mesh):
    in_specs = (
        P(("groups", "blk", "section"), None),
        P(("groups", "blk"), None, None),
        P(("groups", "blk"), None, None),
        P(),
        P(None, "heads"),
        P("heads", None),
        P(),
        P(),
        P("blk", ("heads", "section")),
        P("blk", ("heads", "section")),
        P(("heads", "section"), "blk"),
        P(),
    )
    out_specs = P(("groups", "blk", "heads", "section"), None)
    return jax.shard_map(body, mesh=mesh, in_specs=in_specs, out_specs=out_specs, check_vma=False)
```

profile of v0, /device:TPU:0, one launch (start us, length us, event | category | flops | bytes accessed | tf_op | source)
XLA Modules:
  0.0 725.9 jit_solution(15588221195975664672)
XLA Ops:
  6.5 0.0 copy-start
  6.5 0.0 all-reduce.2.cloned.1.call-start
  6.5 16.0 %all-gather = bf16[512,1,256]{2,0,1:T(8,128)(2,1)S(1)} all-gather(bf16[128,1,256]{2,0,1:T(8,128)(2,1)} %param.13), channel_id=2, replica_groups=mesh['groups'=2,'blk'=4,'heads'=2,'section'=2] {'blk'}, dimensions={0}, use_global_device_ids=true | all-gather | bytes 327680 | tf_op jit(solution)/shard_map/all_gather | solution.py:59
  22.5 1.6 fusion.13
  24.1 14.8 %all-gather.1 = bf16[512,1,256]{2,0,1:T(8,128)(2,1)S(1)} all-gather(bf16[128,1,256]{2,0,1:T(8,128)(2,1)} %param.14), channel_id=3, replica_groups=mesh['groups'=2,'blk'=4,'heads'=2,'section'=2] {'blk'}, dimensions={0}, use_global_device_ids=true | all-gather | bytes 327680 | tf_op jit(solution)/shard_map/all_gather | solution.py:62
  38.9 2.6 fusion.45
  41.4 0.0 copy-done
  41.4 0.0 copy-start.1
  41.5 1.7 convolution_convert_fusion.1
  43.2 0.0 all-reduce.2.cloned.1.call-update
  43.2 0.0 copy-start.2
  43.2 0.0 all-gather.7.cloned.1.call-start
  43.3 43.9 %all-reduce.2.cloned.1.call-done = bf16[256,2304]{1,0:T(8,128)(2,1)} async-done(((bf16[256,2304]{1,0:T(8,128)(2,1)}), bf16[256,2304]{1,0:T(8,128)(2,1)}) %all-reduce.2.cloned.1.call-update) | async-done | bytes 1179664 | tf_op jit(solution)/shard_map/psum | solution.py:68
  87.2 1.6 fusion.8
  88.8 0.0 copy-done.1
  88.8 2.0 fusion.10
  90.8 0.0 copy-done.2
  90.8 1.4 fusion.12
  92.2 0.0 all-gather.7.cloned.1.call-update
  92.2 0.0 all-gather.9.cloned.1.call-start
  92.3 0.7 all-gather.9.cloned.1.call-update
  93.0 0.0 all-gather.11.cloned.1.call-start
  93.0 0.5 all-gather.11.cloned.1.call-update
  93.5 0.0 all-gather.13.cloned.1.call-start
  93.6 0.5 all-gather.13.cloned.1.call-update
  94.1 0.0 reduce-scatter.2.cloned.1.call-start
  94.2 9.2 %all-gather.7.cloned.1.call-done = bf16[512,2304]{1,0:T(8,128)(2,1)} async-done(((bf16[256,2304]{1,0:T(8,128)(2,1)}), bf16[512,2304]{1,0:T(8,128)(2,1)}) %all-gather.7.cloned.1.call-update) | async-done | bytes 2359312 | tf_op jit(solution)/shard_map/all_gather | solution.py:75
  103.3 188.8 %all-gather.9.cloned.1.call-done = bf16[2304,2304]{1,0:T(8,128)(2,1)} async-done(((bf16[576,2304]{1,0:T(8,128)(2,1)}), bf16[2304,2304]{1,0:T(8,128)(2,1)}) %all-gather.9.cloned.1.call-update) | async-done | bytes 10616848 | tf_op jit(solution)/shard_map/all_gather | solution.py:51
  292.2 11.6 %fusion.48 = f32[512,2304]{1,0:T(8,128)} fusion(bf16[512,2304]{1,0:T(8,128)(2,1)} %all-gather.7.cloned.1.call-done, bf16[2304,2304]{1,0:T(8,128)(2,1)} %all-gather.9.cloned.1.call-done), kind=kOutput, calls=%fused_computation.58 | convolution fusion | flops 5435817984 | bytes 17694720 | tf_op jit(solution)/shard_map/dot_general | solution.py:88
  303.8 174.1 %all-gather.11.cloned.1.call-done = bf16[2304,2304]{1,0:T(8,128)(2,1)} async-done(((bf16[576,2304]{1,0:T(8,128)(2,1)}), bf16[2304,2304]{1,0:T(8,128)(2,1)}) %all-gather.11.cloned.1.call-update) | async-done | bytes 10616848 | tf_op jit(solution)/shard_map/all_gather | solution.py:52
  477.8 185.7 %all-gather.13.cloned.1.call-done = bf16[2304,2304]{0,1:T(8,128)(2,1)} async-done(((bf16[2304,576]{0,1:T(8,128)(2,1)}), bf16[2304,2304]{0,1:T(8,128)(2,1)}) %all-gather.13.cloned.1.call-update) | async-done | bytes 10616848 | tf_op jit(solution)/shard_map/all_gather | solution.py:53
  663.5 20.7 %convolution_convert_fusion = bf16[512,2304]{1,0:T(8,128)(2,1)} fusion(bf16[2304,2304]{0,1:T(8,128)(2,1)} %all-gather.13.cloned.1.call-done, bf16[512,2304]{1,0:T(8,128)(2,1)} %all-gather.7.cloned.1.call-done, bf16[2304,2304]{1,0:T(8,128)(2,1)} %all-gather.11.cloned.1.call-done, f32[512,2304]{1,0:T(8,128)} %fusion.48), kind=kOutput, calls=%fused_computation.10 | convolution fusion | flops 10884612096 | bytes 30670848 | tf_op jit(solution)/shard_map/dot_general | solution.py:91
  684.3 0.0 copy-start.3
  684.3 0.0 reduce-scatter.2.cloned.1.call-update
  684.3 0.1 constant_dynamic-slice_fusion
  684.5 0.1 collective-permute-start
  684.6 30.9 %reduce-scatter.2.cloned.1.call-done = bf16[128,2304]{1,0:T(8,128)(2,1)} async-done(((bf16[512,2304]{1,0:T(8,128)(2,1)}), bf16[128,2304]{1,0:T(8,128)(2,1)}) %reduce-scatter.2.cloned.1.call-update) | async-done | bytes 589840 | tf_op jit(solution)/shard_map/reduce_scatter | solution.py:92
  715.4 1.3 fusion.20
  716.7 0.0 collective-permute-done
  716.7 0.0 copy-done.3
  716.7 2.3 fusion.23
  (4 shorter events, 0.0 us)
Async XLA Ops:
  6.5 34.9 %copy-start = (bf16[256,2304]{1,0:T(8,128)(2,1)S(1)}, bf16[256,2304]{1,0:T(8,128)(2,1)}, u32[]{:S(2)}) copy-start(bf16[256,2304]{1,0:T(8,128)(2,1)} %param.17) | copy-start | bytes 3538948
  6.5 80.7 %all-reduce.2.cloned.1.call-start = ((), (), s32[]{:S(2)}) async-start(), calls=%async_computation.1 | async-start | bytes 2359296 | tf_op jit(solution)/shard_map/psum | solution.py:68
  41.4 47.3 %copy-start.1 = (bf16[256,2304]{1,0:T(8,128)(2,1)S(1)}, bf16[256,2304]{1,0:T(8,128)(2,1)}, u32[]{:S(2)}) copy-start(bf16[256,2304]{1,0:T(8,128)(2,1)} %param.12) | copy-start | bytes 3538948
  43.2 47.6 %copy-start.2 = (f32[2304]{0:T(1024)S(1)}, f32[2304]{0:T(1024)}, u32[]{:S(2)}) copy-start(f32[2304]{0:T(1024)} %param.19) | copy-start | bytes 27652
  43.2 60.1 %all-gather.7.cloned.1.call-start = ((), (), s32[]{:S(2)}) async-start(), calls=%async_computation.2 | async-start | bytes 3538944 | tf_op jit(solution)/shard_map/all_gather | solution.py:75
  92.2 199.9 %all-gather.9.cloned.1.call-start = ((), (), s32[]{:S(2)}) async-start(), calls=%async_computation.3 | async-start | bytes 13271040 | tf_op jit(solution)/shard_map/all_gather | solution.py:51
  93.0 384.9 %all-gather.11.cloned.1.call-start = ((), (), s32[]{:S(2)}) async-start(), calls=%async_computation.4 | async-start | bytes 13271040 | tf_op jit(solution)/shard_map/all_gather | solution.py:52
  93.5 570.0 %all-gather.13.cloned.1.call-start = ((), (), s32[]{:S(2)}) async-start(), calls=%async_computation.5 | async-start | bytes 13271040 | tf_op jit(solution)/shard_map/all_gather | solution.py:53
  94.1 621.3 %reduce-scatter.2.cloned.1.call-start = ((), (), s32[]{:S(2)}) async-start(), calls=%async_computation.6 | async-start | bytes 2949120 | tf_op jit(solution)/shard_map/reduce_scatter | solution.py:92
  684.3 32.5 %copy-start.3 = (f32[2304]{0:T(1024)S(1)}, f32[2304]{0:T(1024)}, u32[]{:S(2)}) copy-start(f32[2304]{0:T(1024)} %param.23) | copy-start | bytes 27652
  684.5 32.3 %collective-permute-start = (bf16[128,2304]{1,0:T(8,128)(2,1)S(1)}, bf16[128,2304]{1,0:T(8,128)(2,1)S(1)}, u32[]{:S(2)}, u32[]{:S(2)}) collective-permute-start(bf16[128,2304]{1,0:T(8,128)(2,1)S(1)} %constant_dynamic-slice_fusion), channel_id=1, source_target_pairs={{0,1},{1,0},{2,3},{3,2},{4,5},{5,4},{6,7},{7,6},{8,9},{9,8},{10,11... | collective-permute-start | bytes 1769480 | tf_op jit(solution)/shard_map/ppermute | solution.py:18
Sparse Core Ops, SparseCore 0:
  43.3 43.8 all-reduce.1
  92.3 10.9 all-gather.6
  104.9 187.2 all-gather.8
  293.6 184.2 all-gather.10
  479.3 184.2 all-gather.12
  684.4 30.9 reduce-scatter.1
where the time goes:
time: 726 us
  waiting for transfers between devices  634 us (87%)
  matrix products  36.7 us (5%)
  blocking collectives  30.7 us (4%)
  between operations  13.6 us (2%)
  other arithmetic  10.1 us (1%)
    all_gather x1, waiting for transfers between devices, body(): lax.all_gather(gate_weight, 'blk', axis=0, tiled=True)  189 us
    all_gather x1, waiting for transfers between devices, body(): lax.all_gather(down_weight, 'blk', axis=1, tiled=True)  186 us
    all_gather x1, waiting for transfers between devices, body(): lax.all_gather(up_weight, 'blk', axis=0, tiled=True)  174 us
    psum x1, waiting for transfers between devices, body(): lax.psum(head_term.astype(jnp.bfloat16), 'heads').astype(jnp.float32)  43.9 us
    reduce_scatter x1, waiting for transfers between devices, body(): lax.psum_scatter(terms.astype(jnp.bfloat16), ('heads', 'section'), scatte...  30.9 us
    dot_general x1, matrix products, body(): terms = jnp.dot(hidden, down_full, preferred_element_type=jnp.float32)  20.7 us
    all_gather x1, blocking collectives, body(): lax.all_gather(keys_local, 'blk', axis=0, tiled=True)  16 us
    all_gather x1, blocking collectives, body(): lax.all_gather(values_local, 'blk', axis=0, tiled=True)  14.8 us
  transfers between devices with their start and end apart: 7, of which 6 were waited for; matrix products, arithmetic and copies ran while one was open for 2% of the time, Pallas kernels for 0%

commit v1 on v0

--- a/solution.py
+++ b/solution.py
@@ -6,6 +6,28 @@
 HD = 256
 GROUP = 2
 softcap_limit = 50.0
+
+
+def in_order(pieces, dim):
+    pieces = jnp.moveaxis(pieces, 0, dim)
+    shape = pieces.shape
+    return pieces.reshape(*shape[:dim], shape[dim] * shape[dim + 1], *shape[dim + 2 :])
+
+
+def ring_gather(x, axis, dim):
+    size = lax.axis_size(axis)
+    pairs = [(i, (i + 1) % size) for i in range(size)]
+    back = [(b, a) for a, b in pairs]
+    lower, upper = ([], [])
+    for step in range(size - 1):
+        if step % 2 == 0:
+            lower.append(lax.ppermute(lower[-1] if lower else x, axis, pairs))
+        else:
+            upper.append(lax.ppermute(upper[-1] if upper else x, axis, back))
+    blocks = jnp.stack([*lower[::-1], x, *upper])
+    shift = lax.axis_index(axis) - len(lower)
+    blocks = blocks[(jnp.arange(size) - shift) % size]
+    return in_order(blocks, dim)
 
 
 def from_partner(block, axis, bit):
@@ -50,7 +72,7 @@
     gate_full, up_full, down_full = (
         lax.all_gather(gate_weight, "blk", axis=0, tiled=True),
         lax.all_gather(up_weight, "blk", axis=0, tiled=True),
-        lax.all_gather(down_weight, "blk", axis=1, tiled=True),
+        ring_gather(down_weight, "blk", 1),
     )
     states = dec_states.astype(jnp.float32)
     normed = rms_scale(states, attn_gain).astype(jnp.bfloat16)

time: 726 us -> 687 us (0.946)
  waiting for transfers between devices: 634 us -> 467 us
  starting transfers between devices: 0.27 us -> 87.9 us
  local copies, waits for them, and re-layouts: 0.17 us -> 21.5 us
  other arithmetic: 10.1 us -> 29.1 us
    ppermute x0 -> x3, waiting for transfers between devices: none -> 237 us  [the longest x2 166 us: ring_gather(): lower.append(lax.ppermute(lower[-1] if lower else x, axis, pairs))]
    all_gather x1, waiting for transfers between devices: 189 us -> 0.01 us  [body(): lax.all_gather(gate_weight, 'blk', axis=0, tiled=True)]
    all_gather x1 -> x0, waiting for transfers between devices: 186 us -> none  [body(): lax.all_gather(down_weight, 'blk', axis=1, tiled=True)]
    ppermute x0 -> x3, starting transfers between devices: none -> 87.7 us  [the longest x2 85.4 us: ring_gather(): lower.append(lax.ppermute(lower[-1] if lower else x, axis, pairs))]
    gather x0 -> x3, local copies, waits for them, and re-layouts: none -> 21.3 us  [ring_gather(): blocks = blocks[(jnp.arange(size) - shift) % size]]
    all_gather x1, waiting for transfers between devices: 174 us -> 155 us  [body(): lax.all_gather(up_weight, 'blk', axis=0, tiled=True)]
    unnamed x0 -> x1, other arithmetic: none -> 9.55 us
    another operation x0 -> x1, other arithmetic: none -> 9.43 us  [ring_gather(): blocks = jnp.stack([*lower[::-1], x, *upper])]
  transfers between devices with their start and end apart: 7 -> 9, of which waited for: 6 -> 6; matrix products, arithmetic and copies ran while one was open for 2% -> 8% of each run, Pallas kernels for 0% -> 0%
where the time goes in v1:
time: 687 us; the launch traced here: 686 us
  waiting for transfers between devices  467 us (68%)
  starting transfers between devices  87.9 us (13%)
  matrix products  36.7 us (5%)
  blocking collectives  30.7 us (4%)
  other arithmetic  29.1 us (4%)
  local copies, waits for them, and re-layouts  21.5 us (3%)
  between operations  13.3 us (2%)
    ppermute x2, waiting for transfers between devices, ring_gather(): lower.append(lax.ppermute(lower[-1] if lower else x, axis, pairs))  166 us
    all_gather x1, waiting for transfers between devices, body(): lax.all_gather(up_weight, 'blk', axis=0, tiled=True)  155 us
    ppermute x2, starting transfers between devices, ring_gather(): lower.append(lax.ppermute(lower[-1] if lower else x, axis, pairs))  85.4 us
    ppermute x1, waiting for transfers between devices, ring_gather(): upper.append(lax.ppermute(upper[-1] if upper else x, axis, back))  70.2 us
    psum x1, waiting for transfers between devices, body(): lax.psum(head_term.astype(jnp.bfloat16), 'heads').astype(jnp.float32)  43.9 us
    reduce_scatter x1, waiting for transfers between devices, body(): lax.psum_scatter(terms.astype(jnp.bfloat16), ('heads', 'section'), scatte...  30.9 us
    gather x3, local copies, waits for them, and re-layouts, ring_gather(): blocks = blocks[(jnp.arange(size) - shift) % size]  21.3 us
    dot_general x1, matrix products, body(): terms = jnp.dot(hidden, down_full, preferred_element_type=jnp.float32)  20.8 us
  transfers between devices with their start and end apart: 9, of which 6 were waited for; matrix products, arithmetic and copies ran while one was open for 8% of the time, Pallas kernels for 0%

profile of v1, /device:TPU:0, one launch (start us, length us, event | category | flops | bytes accessed | tf_op | source)
XLA Modules:
  0.0 686.4 jit_solution(5611901723703186765)
XLA Ops:
  6.5 0.0 copy-start
  6.5 0.0 all-reduce.2.cloned.1.call-start
  6.5 16.0 %all-gather = bf16[512,1,256]{2,0,1:T(8,128)(2,1)S(1)} all-gather(bf16[128,1,256]{2,0,1:T(8,128)(2,1)} %param.13), channel_id=2, replica_groups=mesh['groups'=2,'blk'=4,'heads'=2,'section'=2] {'blk'}, dimensions={0}, use_global_device_ids=true | all-gather | bytes 327680 | tf_op jit(solution)/shard_map/all_gather | solution.py:81
  22.5 1.6 fusion.13
  24.1 14.8 %all-gather.1 = bf16[512,1,256]{2,0,1:T(8,128)(2,1)S(1)} all-gather(bf16[128,1,256]{2,0,1:T(8,128)(2,1)} %param.14), channel_id=3, replica_groups=mesh['groups'=2,'blk'=4,'heads'=2,'section'=2] {'blk'}, dimensions={0}, use_global_device_ids=true | all-gather | bytes 327680 | tf_op jit(solution)/shard_map/all_gather | solution.py:84
  38.9 2.6 fusion.48
  41.4 0.0 copy-start.2
  41.4 0.0 copy-start.5
  41.5 0.0 copy-done
  41.5 1.7 convolution_convert_fusion.1
  43.2 0.0 all-reduce.2.cloned.1.call-update
  43.2 0.0 copy-start.3
  43.2 0.0 all-gather.6.cloned.1.call-start
  43.3 43.9 %all-reduce.2.cloned.1.call-done = bf16[256,2304]{1,0:T(8,128)(2,1)} async-done(((bf16[256,2304]{1,0:T(8,128)(2,1)}), bf16[256,2304]{1,0:T(8,128)(2,1)}) %all-reduce.2.cloned.1.call-update) | async-done | bytes 1179664 | tf_op jit(solution)/shard_map/psum | solution.py:90
  87.2 1.6 fusion.8
  88.8 0.0 copy-done.2
  88.8 0.0 copy-done.5
  88.8 2.0 fusion.10
  90.8 0.0 copy-done.3
  90.8 1.4 fusion.12
  92.2 0.0 all-gather.6.cloned.1.call-update
  92.2 0.0 all-gather.8.cloned.1.call-start
  92.3 0.7 all-gather.8.cloned.1.call-update
  92.9 0.0 all-gather.10.cloned.1.call-start
  93.0 0.5 all-gather.10.cloned.1.call-update
  93.5 0.0 reduce-scatter.2.cloned.1.call-start
  93.6 1.5 collective-permute-start.1
  95.1 2.3 collective-permute-start.3
  97.4 94.2 %collective-permute-done.1 = bf16[2304,576]{0,1:T(8,128)(2,1)} collective-permute-done((bf16[2304,576]{0,1:T(8,128)(2,1)}, bf16[2304,576]{0,1:T(8,128)(2,1)}, u32[]{:S(2)}, u32[]{:S(2)}) %collective-permute-start.1) | collective-permute-done | bytes 2654240 | tf_op jit(solution)/shard_map/ppermute | solution.py:24
  191.6 83.8 %collective-permute-start.2 = (bf16[2304,576]{0,1:T(8,128)(2,1)}, bf16[2304,576]{0,1:T(8,128)(2,1)}, u32[]{:S(2)}, u32[]{:S(2)}) collective-permute-start(bf16[2304,576]{0,1:T(8,128)(2,1)} %collective-permute-done.1), channel_id=1, source_target_pairs={{0,4},{4,8},{8,12},{12,0},{1,5},{5,9},{9,13},{13,1},{2,6},{6,10},{... | collective-permute-start | bytes 7962632 | tf_op jit(solution)/shard_map/ppermute | solution.py:24
  275.4 70.2 %collective-permute-done.3 = bf16[2304,576]{0,1:T(8,128)(2,1)} collective-permute-done((bf16[2304,576]{0,1:T(8,128)(2,1)}, bf16[2304,576]{0,1:T(8,128)(2,1)}, u32[]{:S(2)}, u32[]{:S(2)}) %collective-permute-start.3) | collective-permute-done | bytes 2654240 | tf_op jit(solution)/shard_map/ppermute | solution.py:26
  345.6 72.2 %collective-permute-done.2 = bf16[2304,576]{0,1:T(8,128)(2,1)} collective-permute-done((bf16[2304,576]{0,1:T(8,128)(2,1)}, bf16[2304,576]{0,1:T(8,128)(2,1)}, u32[]{:S(2)}, u32[]{:S(2)}) %collective-permute-start.2) | collective-permute-done | bytes 2654240 | tf_op jit(solution)/shard_map/ppermute | solution.py:24
  417.8 9.4 %pad_maximum_fusion = bf16[4,2304,576]{1,2,0:T(8,128)(2,1)} fusion(bf16[1,2304,576]{1,2,0:T(8,128)(2,1)} %bitcast.5, bf16[1,2304,576]{1,2,0:T(8,128)(2,1)} %bitcast.27, bf16[1,2304,576]{1,2,0:T(8,128)(2,1)} %bitcast.3, bf16[1,2304,576]{1,2,0:T(8,128)(2,1)} %bitcast.2), kind=kLoop, calls=%fused_computation.2 | loop fusion | flops 15925248 | bytes 21233664 | tf_op jit(solution)/shard_map/stack | solution.py:27
  427.3 8.9 %fusion.47 = (bf16[4,1152,576]{1,2,0:T(8,128)(2,1)}, bf16[4,1152,576]{1,2,0:T(8,128)(2,1)}) fusion(bf16[4,2304,576]{1,2,0:T(8,128)(2,1)} %pad_maximum_fusion), kind=kLoop, calls=%fused_computation.68 | loop fusion | bytes 21233664 | tf_op jit(solution)/shard_map/gather | solution.py:29
  436.2 6.0 gather_fusion
  442.2 6.4 gather_fusion.1
  448.6 9.6 %pad_maximum_fusion.1 = bf16[4,2304,576]{1,2,0:T(8,128)(2,1)} fusion(bf16[4,1152,576]{1,2,0:T(8,128)(2,1)} %gather_fusion.1, bf16[4,1152,576]{1,2,0:T(8,128)(2,1)} %gather_fusion), kind=kLoop, calls=%fused_computation.3 | loop fusion | flops 21233664 | bytes 21233664
  458.1 0.0 all-gather.6.cloned.1.call-done
  458.1 0.0 all-gather.8.cloned.1.call-done
  458.1 11.7 %fusion.51 = f32[512,2304]{1,0:T(8,128)} fusion(bf16[512,2304]{1,0:T(8,128)(2,1)} %all-gather.6.cloned.1.call-done, bf16[2304,2304]{1,0:T(8,128)(2,1)} %all-gather.8.cloned.1.call-done), kind=kOutput, calls=%fused_computation.70 | convolution fusion | flops 5435817984 | bytes 17694720 | tf_op jit(solution)/shard_map/dot_general | solution.py:110
  469.8 154.5 %all-gather.10.cloned.1.call-done = bf16[2304,2304]{1,0:T(8,128)(2,1)} async-done(((bf16[576,2304]{1,0:T(8,128)(2,1)}), bf16[2304,2304]{1,0:T(8,128)(2,1)}) %all-gather.10.cloned.1.call-update) | async-done | bytes 10616848 | tf_op jit(solution)/shard_map/all_gather | solution.py:74
  624.3 20.8 %convolution_convert_fusion = bf16[512,2304]{1,0:T(8,128)(2,1)} fusion(bf16[2304,2304]{0,1:T(8,128)(2,1)} %bitcast.26, bf16[512,2304]{1,0:T(8,128)(2,1)} %all-gather.6.cloned.1.call-done, bf16[2304,2304]{1,0:T(8,128)(2,1)} %all-gather.10.cloned.1.call-done, f32[512,2304]{1,0:T(8,128)} %fusion.51), kind=kOutput, calls=%fused_computation.14 | convolution fusion | flops 10884612096 | bytes 30670848 | tf_op jit(solution)/shard_map/dot_general | solution.py:113
  645.1 0.0 copy-start.4
  645.1 0.0 reduce-scatter.2.cloned.1.call-update
  645.1 0.0 copy-start.1
  645.1 0.1 constant_dynamic-slice_fusion
  645.3 0.1 collective-permute-start
  645.4 30.9 %reduce-scatter.2.cloned.1.call-done = bf16[128,2304]{1,0:T(8,128)(2,1)} async-done(((bf16[512,2304]{1,0:T(8,128)(2,1)}), bf16[128,2304]{1,0:T(8,128)(2,1)}) %reduce-scatter.2.cloned.1.call-update) | async-done | bytes 589840 | tf_op jit(solution)/shard_map/reduce_scatter | solution.py:114
  676.3 1.3 fusion.20
  677.5 0.0 collective-permute-done
  677.5 0.0 copy-done.4
  677.5 2.3 fusion.23
  679.8 0.0 copy-done.1
  (6 shorter events, 0.1 us)
Async XLA Ops:
  6.5 34.9 %copy-start = (bf16[256,2304]{1,0:T(8,128)(2,1)S(1)}, bf16[256,2304]{1,0:T(8,128)(2,1)}, u32[]{:S(2)}) copy-start(bf16[256,2304]{1,0:T(8,128)(2,1)} %param.17) | copy-start | bytes 3538948
  6.5 80.7 %all-reduce.2.cloned.1.call-start = ((), (), s32[]{:S(2)}) async-start(), calls=%async_computation.1 | async-start | bytes 2359296 | tf_op jit(solution)/shard_map/psum | solution.py:90
  41.4 47.4 %copy-start.2 = (bf16[256,2304]{1,0:T(8,128)(2,1)S(1)}, bf16[256,2304]{1,0:T(8,128)(2,1)}, u32[]{:S(2)}) copy-start(bf16[256,2304]{1,0:T(8,128)(2,1)} %param.12) | copy-start | bytes 3538948
  41.4 47.4 %copy-start.5 = (f32[2304]{0:T(1024)S(1)}, f32[2304]{0:T(1024)}, u32[]{:S(2)}) copy-start(f32[2304]{0:T(1024)} %param.18) | copy-start | bytes 27652
  43.2 47.6 %copy-start.3 = (f32[2304]{0:T(1024)S(1)}, f32[2304]{0:T(1024)}, u32[]{:S(2)}) copy-start(f32[2304]{0:T(1024)} %param.19) | copy-start | bytes 27652
  43.2 414.9 %all-gather.6.cloned.1.call-start = ((), (), s32[]{:S(2)}) async-start(), calls=%async_computation.2 | async-start | bytes 3538944 | tf_op jit(solution)/shard_map/all_gather | solution.py:97
  92.2 365.9 %all-gather.8.cloned.1.call-start = ((), (), s32[]{:S(2)}) async-start(), calls=%async_computation.3 | async-start | bytes 13271040 | tf_op jit(solution)/shard_map/all_gather | solution.py:73
  92.9 531.4 %all-gather.10.cloned.1.call-start = ((), (), s32[]{:S(2)}) async-start(), calls=%async_computation.4 | async-start | bytes 13271040 | tf_op jit(solution)/shard_map/all_gather | solution.py:74
  93.5 582.7 %reduce-scatter.2.cloned.1.call-start = ((), (), s32[]{:S(2)}) async-start(), calls=%async_computation.5 | async-start | bytes 2949120 | tf_op jit(solution)/shard_map/reduce_scatter | solution.py:114
  93.6 98.0 %collective-permute-start.1 = (bf16[2304,576]{0,1:T(8,128)(2,1)}, bf16[2304,576]{0,1:T(8,128)(2,1)}, u32[]{:S(2)}, u32[]{:S(2)}) collective-permute-start(bf16[2304,576]{0,1:T(8,128)(2,1)} %param.22), channel_id=1, source_target_pairs={{0,4},{4,8},{8,12},{12,0},{1,5},{5,9},{9,13},{13,1},{2,6},{6,10},{... | collective-permute-start | bytes 7962632 | tf_op jit(solution)/shard_map/ppermute | solution.py:24
  95.1 250.5 %collective-permute-start.3 = (bf16[2304,576]{0,1:T(8,128)(2,1)}, bf16[2304,576]{0,1:T(8,128)(2,1)}, u32[]{:S(2)}, u32[]{:S(2)}) collective-permute-start(bf16[2304,576]{0,1:T(8,128)(2,1)} %param.22), channel_id=1, source_target_pairs={{4,0},{8,4},{12,8},{0,12},{5,1},{9,5},{13,9},{1,13},{6,2},{10,6},{... | collective-permute-start | bytes 7962632 | tf_op jit(solution)/shard_map/ppermute | solution.py:26
  191.6 226.2 %collective-permute-start.2 = (bf16[2304,576]{0,1:T(8,128)(2,1)}, bf16[2304,576]{0,1:T(8,128)(2,1)}, u32[]{:S(2)}, u32[]{:S(2)}) collective-permute-start(bf16[2304,576]{0,1:T(8,128)(2,1)} %collective-permute-done.1), channel_id=1, source_target_pairs={{0,4},{4,8},{8,12},{12,0},{1,5},{5,9},{9,13},{13,1},{2,6},{6,10},{... | collective-permute-start | bytes 7962632 | tf_op jit(solution)/shard_map/ppermute | solution.py:24
  645.1 32.5 %copy-start.4 = (f32[2304]{0:T(1024)S(1)}, f32[2304]{0:T(1024)}, u32[]{:S(2)}) copy-start(f32[2304]{0:T(1024)} %param.23) | copy-start | bytes 27652
  645.1 34.7 %copy-start.1 = (bf16[256,2304]{1,0:T(8,128)(2,1)S(1)}, bf16[256,2304]{1,0:T(8,128)(2,1)}, u32[]{:S(2)}) copy-start(bf16[256,2304]{1,0:T(8,128)(2,1)} %param.17) | copy-start | bytes 3538948
  645.3 32.2 %collective-permute-start = (bf16[128,2304]{1,0:T(8,128)(2,1)S(1)}, bf16[128,2304]{1,0:T(8,128)(2,1)S(1)}, u32[]{:S(2)}, u32[]{:S(2)}) collective-permute-start(bf16[128,2304]{1,0:T(8,128)(2,1)S(1)} %constant_dynamic-slice_fusion), channel_id=1, source_target_pairs={{0,1},{1,0},{2,3},{3,2},{4,5},{5,4},{6,7},{7,6},{8,9},{9,8},{10,11... | collective-permute-start | bytes 1769480 | tf_op jit(solution)/shard_map/ppermute | solution.py:40
Sparse Core Ops, SparseCore 0:
  43.3 43.8 all-reduce.1
  92.3 10.9 all-gather.5
  104.9 334.5 all-gather.7
  440.9 183.3 all-gather.9
  645.2 30.9 reduce-scatter.1
